TPU v7x, 128 devices: a whole 4x4x4 slice. The times are simulated.
128 devices in a mesh: req: 32 (over z, y, x_lo), exp: 4 (over x_hi, core).
Axes of the slice: x: 4 (x_hi: 2, x_lo: 2; x = x_hi * 2 + x_lo), y: 4, z: 4, core: 2. Of those that a mesh axis runs over, the one named last changes fastest.
Arguments:
- hidden_in: bfloat16 [8192, 2048], P(('req', 'exp')), may hold values from -6 to 6
- query_in: bfloat16 [8192, 2048], P('req', 'exp'), may hold values from -6 to 6
- key_in: bfloat16 [8192, 2048], P('req', 'exp'), may hold values from -6 to 6
- value_in: bfloat16 [8192, 2048], P('req', 'exp'), may hold values from -24 to 24
- query_gain: float32 [128], replicated, may hold values from 0.5 to 2.5
- key_gain: float32 [128], replicated, may hold values from 0.5 to 2.5
- cache_keys: bfloat16 [64, 32, 2048], P('req', None, 'exp'), may hold values from -400 to 400
- cache_values: bfloat16 [64, 32, 2048], P('req', None, 'exp'), may hold values from -24 to 24
- cache_block: int32 [128], replicated, may hold values from -1 to 63, as said below
- request_lengths: int32 [32, 4], P('req'), may hold values from 1 to 128, 256 in all within a row
- out_proj: bfloat16 [2048, 2048], P('exp'), may hold values from -0.125 to 0.125
- norm_gain: float32 [2048], replicated, may hold values from 0.25 to 1.75
- expert_ids: int32 [8192, 8], P(('req', 'exp')), may hold values from 0 to 63, all different within a row; in each aligned block of 64 rows (0 to 63, 64 to 127, ...) at most 10 rows name the same one
- gate_values: float32 [8192, 8], P(('req', 'exp')), may hold values from 0.4 to 1.6
- old_slots: int32 [64], replicated, may hold values from 0 to 63, each once
- new_replicas: int32 [32], replicated, may hold values from 0 to 63
- slot_weights: bfloat16 [64, 3, 2048, 1024], P('req', None, None, 'exp'), may hold values from -0.125 to 0.125
Outputs:
- layer_out: bfloat16 [8192, 2048], P(('req', 'exp'))
- replica_weights: bfloat16 [32, 3, 2048, 1024], P('req', None, None, 'exp')
Inputs may be any that keep to these rules, and one draw needn't show every extreme that they name: `cache_block`: each index of req has exactly 2 of its 4 requests with a block; every block serves exactly one request. `expert_ids`: in each aligned block of 64 rows (the rows of one device) no expert is named by more than 10 rows, a bound that some block reaches; the 8 experts of a row differ. `old_slots`: every expert is in exactly one slot. `request_lengths`: the lengths of each index of req sum to 256.
All inputs are finite; a program needn't handle non-finite values.
Results may differ from a plain program's by a relative error of at most 0.025.
Values may be sent and summed in bfloat16 or wider, within the bound.
A program may use at most 128 MiB of HBM per device.

v0:
```python
import math
import jax
import jax.numpy as jnp
from jax import lax
from jax.sharding import PartitionSpec as P


def prepare(values, gain, position):
    vector = values.astype(jnp.float32)
    scaled = vector * lax.rsqrt(jnp.mean(vector * vector, axis=-1, keepdims=True) + 1e-06) * gain
    half_size = scaled.shape[-1] // 2
    frequency = 10000.0 ** (-(jnp.arange(half_size, dtype=jnp.float32) * 2.0 / scaled.shape[-1]))
    angles = position[:, None] * frequency[None, :]
    cosine = jnp.cos(angles)[:, None, :]
    sine_part = jnp.sin(angles)[:, None, :]
    lower_half = scaled[..., :half_size]
    upper_half = scaled[..., half_size:]
    rotated = jnp.concatenate(
        [
            lower_half * cosine - upper_half * sine_part,
            upper_half * cosine + lower_half * sine_part,
        ],
        axis=-1,
    )
    return rotated.astype(jnp.bfloat16)


def compact(block_rows, slots_wanted):
    live = block_rows >= 0
    ranks = jnp.cumsum(live.astype(jnp.int32), axis=1) - 1
    request_idx = jnp.arange(block_rows.shape[1], dtype=jnp.int32)[None, :]
    chosen_blocks = []
    chosen_requests = []
    for slot_num in range(slots_wanted):
        picked = live & (ranks == slot_num)
        chosen_blocks.append(jnp.sum(jnp.where(picked, block_rows, 0), axis=1))
        chosen_requests.append(jnp.sum(jnp.where(picked, request_idx, 0), axis=1))
    return (jnp.stack(chosen_blocks, axis=1), jnp.stack(chosen_requests, axis=1))


def run_slots(inbox, slot_weights, capacity):
    sources = inbox.shape[0]
    model_width = inbox.shape[2]
    slot_count = slot_weights.shape[0]
    grouped = inbox.reshape(sources, slot_count, capacity, model_width)
    results = []
    for slot_num in range(slot_count):
        in_rows = grouped[:, slot_num].reshape(sources * capacity, model_width)
        gate_act = jnp.dot(in_rows, slot_weights[slot_num, 0], preferred_element_type=jnp.float32)
        up_act = jnp.dot(in_rows, slot_weights[slot_num, 1], preferred_element_type=jnp.float32)
        hidden = (jax.nn.silu(gate_act) * up_act).astype(jnp.bfloat16)
        partial_value = lax.dot_general(
            hidden,
            slot_weights[slot_num, 2],
            (((1,), (1,)), ((), ())),
            preferred_element_type=jnp.float32,
        )
        results.append(partial_value.reshape(sources, capacity, model_width))
    return jnp.stack(results, axis=1).reshape(sources, slot_count * capacity, model_width)


def body(
    hidden_in,
    query_in,
    key_in,
    value_in,
    query_gain,
    key_gain,
    cache_keys,
    cache_values,
    cache_block,
    request_lengths,
    out_proj,
    norm_gain,
    expert_ids,
    gate_values,
    old_slots,
    new_replicas,
    slot_weights,
):
    req_count = lax.axis_size("req")
    exp_count = lax.axis_size("exp")
    group_idx = lax.axis_index("req")
    tok_grp, width_q = query_in.shape
    tok_dev, model_width = hidden_in.shape
    head_size = query_gain.shape[0]
    head_count = width_q // head_size
    cache_dev = cache_keys.shape[0]
    pre_len = cache_keys.shape[1]
    req_grp = request_lengths.shape[1]
    lengths = request_lengths[0]
    req_ends = jnp.cumsum(lengths)
    starts = req_ends - lengths
    places = jnp.arange(tok_grp, dtype=jnp.int32)
    member = (places[:, None] >= starts[None, :]) & (places[:, None] < req_ends[None, :])
    request_idx = jnp.arange(req_grp, dtype=jnp.int32)
    segment = jnp.sum(jnp.where(member, request_idx[None, :], 0), axis=1)
    offset = places - jnp.sum(jnp.where(member, starts[None, :], 0), axis=1)
    block_rows = cache_block.reshape(req_count, req_grp)
    my_blocks = lax.dynamic_index_in_dim(block_rows, group_idx, 0, keepdims=False)
    has_cache = my_blocks >= 0
    token_cached = jnp.sum(jnp.where(member & has_cache[None, :], 1, 0), axis=1) > 0
    position = (offset + jnp.where(token_cached, pre_len, 0)).astype(jnp.float32)
    need_blocks, need_requests = compact(block_rows, cache_dev)
    my_requests = lax.dynamic_index_in_dim(need_requests, group_idx, 0, keepdims=False)
    key_width = cache_keys.shape[2]
    rows_per = pre_len // req_count
    both = jnp.concatenate([cache_keys, cache_values], axis=-1)
    both = both.reshape(cache_dev, req_count, rows_per, 2 * key_width).transpose(1, 0, 2, 3)
    spread = lax.all_to_all(both, "req", split_axis=0, concat_axis=0, tiled=True)
    spread = spread.reshape(req_count * cache_dev, rows_per, 2 * key_width)
    picked = jnp.take(spread, need_blocks.reshape(-1), axis=0)
    picked = picked.reshape(req_count, cache_dev, rows_per, 2 * key_width)
    gathered = lax.all_to_all(picked, "req", split_axis=0, concat_axis=0, tiled=True)
    gathered = gathered.transpose(1, 0, 2, 3).reshape(cache_dev, pre_len, 2 * key_width)
    far_keys = gathered[..., :key_width]
    far_values = gathered[..., key_width:]
    query_n = prepare(query_in.reshape(tok_grp, head_count, head_size), query_gain, position)
    key_n = prepare(key_in.reshape(tok_grp, head_count, head_size), key_gain, position)
    keyset = jnp.concatenate(
        [key_n, far_keys.reshape(cache_dev * pre_len, head_count, head_size)], axis=0
    )
    valueset = jnp.concatenate(
        [
            value_in.reshape(tok_grp, head_count, head_size),
            far_values.reshape(cache_dev * pre_len, head_count, head_size),
        ],
        axis=0,
    )
    key_request = jnp.concatenate([segment, jnp.repeat(my_requests, pre_len)])
    allowed = segment[:, None] == key_request[None, :]
    scores = jnp.einsum("qhd,khd->hqk", query_n, keyset, preferred_element_type=jnp.float32) * (
        1.0 / math.sqrt(head_size)
    )
    scores = jnp.where(allowed[None], scores, -1e30)
    peak = jnp.max(scores, axis=-1, keepdims=True)
    expos = jnp.exp(scores - peak)
    weights = (expos / jnp.sum(expos, axis=-1, keepdims=True)).astype(jnp.bfloat16)
    attended = jnp.einsum("hqk,khd->qhd", weights, valueset, preferred_element_type=jnp.float32)
    attended = attended.astype(jnp.bfloat16).reshape(tok_grp, width_q)
    attn_out = lax.psum_scatter(
        jnp.dot(attended, out_proj, preferred_element_type=jnp.float32),
        "exp",
        scatter_dimension=0,
        tiled=True,
    )
    residual = hidden_in.astype(jnp.float32) + attn_out
    normed = (
        residual
        * lax.rsqrt(jnp.mean(residual * residual, axis=-1, keepdims=True) + 1e-06)
        * norm_gain
    ).astype(jnp.bfloat16)
    topk_count = expert_ids.shape[1]
    slot_total = old_slots.shape[0]
    slots_here = slot_weights.shape[0]
    capacity = max(2, tok_dev * topk_count * 5 // (4 * slot_total))
    slot_range = jnp.arange(slot_total, dtype=jnp.int32)
    slot_of = jnp.sum(
        jnp.where(old_slots[None, :] == slot_range[:, None], slot_range[None, :], 0), axis=1
    )
    flat_ids = expert_ids.reshape(-1)
    onehot = flat_ids[:, None] == slot_range[None, :]
    row_slot = jnp.sum(jnp.where(onehot, slot_of[None, :], 0), axis=1)
    before = jnp.cumsum(onehot.astype(jnp.int32), axis=0) - onehot.astype(jnp.int32)
    row_rank = jnp.sum(jnp.where(onehot, before, 0), axis=1)
    target = row_slot * capacity + row_rank
    send_rows = jnp.repeat(normed, topk_count, axis=0)
    outbox = jnp.zeros((slot_total * capacity, model_width), jnp.bfloat16).at[target].set(send_rows)
    outbox = outbox.reshape(req_count, slots_here * capacity, model_width)
    copies = jnp.broadcast_to(
        outbox[:, None], (req_count, exp_count, slots_here * capacity, model_width)
    )
    copies = copies.reshape(req_count * exp_count, slots_here * capacity, model_width)
    inbox = lax.all_to_all(copies, ("req", "exp"), split_axis=0, concat_axis=0, tiled=True)
    partial_value = run_slots(inbox, slot_weights, capacity).astype(jnp.bfloat16)
    returned = lax.all_to_all(
        partial_value, ("req", "exp"), split_axis=0, concat_axis=0, tiled=True
    )
    result = jnp.sum(
        returned.astype(jnp.float32).reshape(
            req_count, exp_count, slots_here * capacity, model_width
        ),
        axis=1,
    )
    result_rows = jnp.take(result.reshape(slot_total * capacity, model_width), target, axis=0)
    mixture = jnp.sum(
        result_rows.reshape(tok_dev, topk_count, model_width) * gate_values[:, :, None], axis=1
    )
    layer_out = (residual + mixture).astype(jnp.bfloat16)
    spread_slots = lax.all_to_all(slot_weights, "req", split_axis=2, concat_axis=0, tiled=True)
    replica_onehot = new_replicas[:, None] == slot_range[None, :]
    source_slot = jnp.sum(jnp.where(replica_onehot, slot_of[None, :], 0), axis=1)
    chosen_pieces = jnp.take(spread_slots, source_slot, axis=0)
    replica_weights = lax.all_to_all(chosen_pieces, "req", split_axis=0, concat_axis=2, tiled=True)
    return (layer_out, replica_weights)


def solution(mesh):
    in_specs = (
        P(("req", "exp"), None),
        P("req", "exp"),
        P("req", "exp"),
        P("req", "exp"),
        P(),
        P(),
        P("req", None, "exp"),
        P("req", None, "exp"),
        P(),
        P("req", None),
        P("exp", None),
        P(),
        P(("req", "exp"), None),
        P(("req", "exp"), None),
        P(),
        P(),
        P("req", None, None, "exp"),
    )
    out_specs = (P(("req", "exp"), None), P("req", None, None, "exp"))
    return jax.shard_map(body, mesh=mesh, in_specs=in_specs, out_specs=out_specs, check_vma=False)
```

profile of v0, /device:TPU:74, one launch (start us, length us, event | category | flops | bytes accessed | tf_op | source)
XLA Modules:
  0.0 696.7 jit_solution(8149768700036297165)
XLA Ops:
  9.9 8.5 %all-to-all-start = ((bf16[32,2,1,1024]{3,1,2,0:T(2,128)(2,1)}), bf16[32,2,1,1024]{3,1,2,0:T(2,128)(2,1)S(1)}, u32[]{:S(2)}, u32[]{:S(2)}) async-start(bf16[32,2,1,1024]{3,1,2,0:T(2,128)(2,1)} %maximum_bitcast_fusion), calls=%async_computation | async-start | bytes 262144 | tf_op jit(solution)/shard_map/all_to_all | solution.py:110
  33.1 10.5 %copy.125 = bf16[2,3,2048,256]{3,1,0,2:T(4,128)(2,1)} copy(bf16[2,3,2048,256]{3,2,1,0:T(8,128)(2,1)} %param.33) | data formatting | bytes 12582912 | tf_op args[16]
  45.2 8.3 %all-to-all-start.1 = ((bf16[32,2,1,1024]{3,1,2,0:T(2,128)(2,1)}), bf16[32,2,1,1024]{3,1,2,0:T(2,128)(2,1)S(1)}, u32[]{:S(2)}, u32[]{:S(2)}) async-start(bf16[32,2,1,1024]{3,1,2,0:T(2,128)(2,1)} %broadcast_select_fusion.1), calls=%async_computation.1 | async-start | bytes 262144 | tf_op jit(solution)/shard_map/all_to_all | solution.py:114
  53.7 4.9 all-to-all-done.1
  58.6 8.6 %all-to-all-start.4 = ((bf16[2,3,2048,256]{3,1,0,2:T(4,128)(2,1)}), bf16[2,3,2048,256]{3,1,0,2:T(4,128)(2,1)}, u32[]{:S(2)}, u32[]{:S(2)}) async-start(bf16[2,3,2048,256]{3,1,0,2:T(4,128)(2,1)} %copy.125), calls=%async_computation.5 | async-start | bytes 16777216 | tf_op jit(solution)/shard_map/all_to_all | solution.py:190
  76.2 47.9 %reduce-scatter.2.cloned.1.call-done = f32[64,2048]{1,0:T(8,128)} async-done(((f32[256,2048]{1,0:T(8,128)}), f32[64,2048]{1,0:T(8,128)}) %reduce-scatter.2.cloned.1.call-update) | async-done | bytes 524304 | tf_op jit(solution)/shard_map/reduce_scatter | solution.py:141
  126.5 5.5 scatter_custom_fusion
  131.9 5.1 broadcast_in_dim.198
  137.1 37.6 %all-to-all-done.4 = bf16[2,3,2048,256]{3,1,0,2:T(4,128)(2,1)} async-done(((bf16[2,3,2048,256]{3,1,0,2:T(4,128)(2,1)}), bf16[2,3,2048,256]{3,1,0,2:T(4,128)(2,1)}, u32[]{:S(2)}, u32[]{:S(2)}) %all-to-all-start.4) | async-done | bytes 6291488 | tf_op jit(solution)/shard_map/all_to_all | solution.py:190
  174.7 8.1 %broadcast_in_dim.199 = bf16[32,4,20,2048]{3,2,1,0:T(8,128)(2,1)} broadcast(bf16[32,20,2048]{2,1,0:T(8,128)(2,1)} %broadcast_in_dim.198), dimensions={0,2,3} | broadcast | bytes 13107200 | tf_op jit(solution)/shard_map/broadcast_in_dim | solution.py:170
  182.8 20.8 %all-to-all-start.2 = ((bf16[128,20,2048]{2,1,0:T(8,128)(2,1)}), bf16[128,20,2048]{2,1,0:T(8,128)(2,1)}, u32[]{:S(2)}, u32[]{:S(2)}) async-start(bf16[128,20,2048]{2,1,0:T(8,128)(2,1)} %bitcast.121), calls=%async_computation.3 | async-start | bytes 25165824 | tf_op jit(solution)/shard_map/all_to_all | solution.py:174
  203.9 4.9 copy.126
  212.1 5.2 gather_fusion.2
  221.2 144.9 %all-to-all-done.2 = bf16[128,20,2048]{2,1,0:T(8,128)(2,1)} async-done(((bf16[128,20,2048]{2,1,0:T(8,128)(2,1)}), bf16[128,20,2048]{2,1,0:T(8,128)(2,1)}, u32[]{:S(2)}, u32[]{:S(2)}) %all-to-all-start.2) | async-done | bytes 10485792 | tf_op jit(solution)/shard_map/all_to_all | solution.py:174
  366.2 7.2 %all-to-all-start.5 = ((bf16[32,3,64,256]{3,2,1,0:T(8,128)(2,1)}), bf16[32,3,64,256]{3,2,1,0:T(8,128)(2,1)}, u32[]{:S(2)}, u32[]{:S(2)}) async-start(bf16[32,3,64,256]{3,2,1,0:T(8,128)(2,1)} %broadcast_select_fusion), calls=%async_computation.6 | async-start | bytes 6291456 | tf_op jit(solution)/shard_map/all_to_all | solution.py:194
  373.4 12.7 %copy.116 = bf16[128,20,2048]{2,0,1:T(8,128)(2,1)} copy(bf16[128,20,2048]{2,1,0:T(8,128)(2,1)} %all-to-all-done.2) | data formatting | bytes 20971520 | tf_op jit(solution)/shard_map/all_to_all | solution.py:174
  386.0 10.2 %fusion.65 = (bf16[128,1,10,2048]{3,0,2,1:T(8,128)(2,1)}, bf16[128,1,10,2048]{3,0,2,1:T(8,128)(2,1)}) fusion(bf16[128,2,10,2048]{3,0,2,1:T(8,128)(2,1)} %bitcast.122), kind=kLoop, calls=%fused_computation.134 | loop fusion | bytes 20971520 | tf_op jit(solution)/shard_map/slice | solution.py:48
  396.3 9.0 %copy.117 = bf16[128,1,10,2048]{3,2,0,1:T(8,128)(2,1)} copy(bf16[128,1,10,2048]{3,0,2,1:T(8,128)(2,1)} %get-tuple-element.13) | data formatting | bytes 10485760 | tf_op jit(solution)/shard_map/slice | solution.py:48
  405.3 9.8 %reshape_squeeze.6 = bf16[1280,2048]{1,0:T(8,128)(2,1)} reshape(bf16[128,1,10,2048]{3,2,0,1:T(8,128)(2,1)} %copy.117) | data formatting | bytes 10485760 | tf_op jit(solution)/shard_map/reshape;squeeze | solution.py:48
  415.1 4.5 fusion.17
  422.8 9.0 %copy.119 = bf16[128,1,10,2048]{3,2,0,1:T(8,128)(2,1)} copy(bf16[128,1,10,2048]{3,0,2,1:T(8,128)(2,1)} %get-tuple-element.14) | data formatting | bytes 10485760 | tf_op jit(solution)/shard_map/slice | solution.py:48
  431.8 10.2 %reshape_squeeze.7 = bf16[1280,2048]{1,0:T(8,128)(2,1)} reshape(bf16[128,1,10,2048]{3,2,0,1:T(8,128)(2,1)} %copy.119) | data formatting | bytes 10485760 | tf_op jit(solution)/shard_map/reshape;squeeze | solution.py:48
  442.0 4.5 fusion.14
  449.7 5.0 convert_bitcast_fusion.1
  454.8 5.2 convert_bitcast_fusion
  459.9 9.0 %pad_maximum_fusion = bf16[128,2,10,2048]{3,0,2,1:T(8,128)(2,1)} fusion(bf16[128,1,10,2048]{3,0,2,1:T(8,128)(2,1)} %convert_bitcast_fusion, bf16[128,1,10,2048]{3,0,2,1:T(8,128)(2,1)} %convert_bitcast_fusion.1), kind=kLoop, calls=%fused_computation.6 | loop fusion | flops 5242880 | bytes 20971520 | tf_op jit(solution)/shard_map/stack | solution.py:59
  468.9 14.0 %copy.121 = bf16[128,20,2048]{2,1,0:T(8,128)(2,1)} copy(bf16[128,20,2048]{2,0,1:T(8,128)(2,1)} %bitcast.123) | data formatting | bytes 20971520 | tf_op jit(solution)/shard_map/convert_element_type | solution.py:175
  482.9 10.9 %all-to-all-start.3 = ((bf16[128,20,2048]{2,1,0:T(8,128)(2,1)}), bf16[128,20,2048]{2,1,0:T(8,128)(2,1)}, u32[]{:S(2)}, u32[]{:S(2)}) async-start(bf16[128,20,2048]{2,1,0:T(8,128)(2,1)} %copy.121), calls=%async_computation.4 | async-start | bytes 25165824 | tf_op jit(solution)/shard_map/all_to_all | solution.py:176
  498.0 160.7 %all-to-all-done.3 = bf16[128,20,2048]{2,1,0:T(8,128)(2,1)} async-done(((bf16[128,20,2048]{2,1,0:T(8,128)(2,1)}), bf16[128,20,2048]{2,1,0:T(8,128)(2,1)}, u32[]{:S(2)}, u32[]{:S(2)}) %all-to-all-start.3) | async-done | bytes 10485792 | tf_op jit(solution)/shard_map/all_to_all | solution.py:176
  658.8 11.1 %convert_reduce_fusion = f32[32,20,2048]{2,1,0:T(8,128)} fusion(bf16[128,20,2048]{2,1,0:T(8,128)(2,1)} %all-to-all-done.3), kind=kLoop, calls=%fused_computation.5 | loop fusion | flops 9175040 | bytes 15728640 | tf_op jit(solution)/shard_map/reduce_sum | solution.py:179
  669.9 6.8 reshape.362
  676.7 8.1 %gather_fusion.1 = f32[512,2048]{1,0:T(8,128)} fusion(f32[640,2048]{1,0:T(8,128)} %reshape.362, s32[1024]{0:T(1024)S(1)} %pad_clamp_fusion.1), kind=kCustom, calls=%fused_computation.1 | custom fusion | bytes 8390656 | tf_op jit(solution)/shard_map/jit(_take)/gather | solution.py:185
  (118 shorter events, 53.0 us)
Async XLA Ops:
  7.2 64.9 %copy-start = (bf16[512,2048]{1,0:T(8,128)(2,1)S(1)}, bf16[512,2048]{1,0:T(8,128)(2,1)}, u32[]{:S(2)}) copy-start(bf16[512,2048]{1,0:T(8,128)(2,1)} %param.27) | copy-start | bytes 6291460
  9.9 33.6 %all-to-all-start = ((bf16[32,2,1,1024]{3,1,2,0:T(2,128)(2,1)}), bf16[32,2,1,1024]{3,1,2,0:T(2,128)(2,1)S(1)}, u32[]{:S(2)}, u32[]{:S(2)}) async-start(bf16[32,2,1,1024]{3,1,2,0:T(2,128)(2,1)} %maximum_bitcast_fusion), calls=%async_computation | async-start | bytes 262144 | tf_op jit(solution)/shard_map/all_to_all | solution.py:110
  20.1 4.2 copy-start.9
  26.9 4.8 copy-start.10
  33.1 10.5 %copy-start.11 = (s32[64]{0:T(128)S(1)}, s32[64]{0:T(128)}, u32[]{:S(2)}) copy-start(s32[64]{0:T(128)} %fusion.50) | copy-start | bytes 772
  45.2 13.3 %all-to-all-start.1 = ((bf16[32,2,1,1024]{3,1,2,0:T(2,128)(2,1)}), bf16[32,2,1,1024]{3,1,2,0:T(2,128)(2,1)S(1)}, u32[]{:S(2)}, u32[]{:S(2)}) async-start(bf16[32,2,1,1024]{3,1,2,0:T(2,128)(2,1)} %broadcast_select_fusion.1), calls=%async_computation.1 | async-start | bytes 262144 | tf_op jit(solution)/shard_map/all_to_all | solution.py:114
  58.6 116.1 %all-to-all-start.4 = ((bf16[2,3,2048,256]{3,1,0,2:T(4,128)(2,1)}), bf16[2,3,2048,256]{3,1,0,2:T(4,128)(2,1)}, u32[]{:S(2)}, u32[]{:S(2)}) async-start(bf16[2,3,2048,256]{3,1,0,2:T(4,128)(2,1)} %copy.125), calls=%async_computation.5 | async-start | bytes 16777216 | tf_op jit(solution)/shard_map/all_to_all | solution.py:190
  67.2 56.9 %reduce-scatter.2.cloned.1.call-start = ((), (), s32[]{:S(2)}) async-start(), calls=%async_computation.7 | async-start | bytes 2621440 | tf_op jit(solution)/shard_map/reduce_scatter | solution.py:141
  72.0 2.1 copy-start.7
  72.0 3.9 copy-start.12
  72.0 52.1 %copy-start.5 = (bf16[64,2048]{1,0:T(8,128)(2,1)S(1)}, bf16[64,2048]{1,0:T(8,128)(2,1)}, u32[]{:S(2)}) copy-start(bf16[64,2048]{1,0:T(8,128)(2,1)} %param.17) | copy-start | bytes 786436
  72.0 53.3 %copy-start.6 = (f32[2048]{0:T(1024)S(1)}, f32[2048]{0:T(1024)}, u32[]{:S(2)}) copy-start(f32[2048]{0:T(1024)} %param.28) | copy-start | bytes 24580
  182.8 20.9 %copy-start.13 = (s32[32]{0:T(128)S(1)}, s32[32]{0:T(128)}, u32[]{:S(2)}) copy-start(s32[32]{0:T(128)} %param.32) | copy-start | bytes 388
  182.8 183.4 %all-to-all-start.2 = ((bf16[128,20,2048]{2,1,0:T(8,128)(2,1)}), bf16[128,20,2048]{2,1,0:T(8,128)(2,1)}, u32[]{:S(2)}, u32[]{:S(2)}) async-start(bf16[128,20,2048]{2,1,0:T(8,128)(2,1)} %bitcast.121), calls=%async_computation.3 | async-start | bytes 25165824 | tf_op jit(solution)/shard_map/all_to_all | solution.py:174
  366.2 116.8 %all-to-all-start.5 = ((bf16[32,3,64,256]{3,2,1,0:T(8,128)(2,1)}), bf16[32,3,64,256]{3,2,1,0:T(8,128)(2,1)}, u32[]{:S(2)}, u32[]{:S(2)}) async-start(bf16[32,3,64,256]{3,2,1,0:T(8,128)(2,1)} %broadcast_select_fusion), calls=%async_computation.6 | async-start | bytes 6291456 | tf_op jit(solution)/shard_map/all_to_all | solution.py:194
  415.1 4.5 copy-start.2
  442.0 4.5 copy-start.3
  482.9 11.0 %copy-start.8 = (f32[64,8]{0,1:T(8,128)S(1)}, f32[64,8]{0,1:T(8,128)}, u32[]{:S(2)}) copy-start(f32[64,8]{0,1:T(8,128)} %param.30) | copy-start | bytes 6148
  482.9 175.8 %all-to-all-start.3 = ((bf16[128,20,2048]{2,1,0:T(8,128)(2,1)}), bf16[128,20,2048]{2,1,0:T(8,128)(2,1)}, u32[]{:S(2)}, u32[]{:S(2)}) async-start(bf16[128,20,2048]{2,1,0:T(8,128)(2,1)} %copy.121), calls=%async_computation.4 | async-start | bytes 25165824 | tf_op jit(solution)/shard_map/all_to_all | solution.py:176
  676.7 13.0 %copy-start.1 = (bf16[512,2048]{1,0:T(8,128)(2,1)S(1)}, bf16[512,2048]{1,0:T(8,128)(2,1)}, u32[]{:S(2)}) copy-start(bf16[512,2048]{1,0:T(8,128)(2,1)} %param.27) | copy-start | bytes 6291460
  684.8 4.1 copy-start.4
Sparse Core Ops, SparseCore 0:
  74.2 49.7 reduce-scatter.1
where the time goes:
time: 704 us; the launch traced here: 697 us
  waiting for transfers between devices  396 us (56%)
  local copies, waits for them, and re-layouts  146 us (21%)
  starting transfers between devices  64.6 us (9%)
  other arithmetic  43.5 us (6%)
  matrix products  31.5 us (4%)
  between operations  14.8 us (2%)
    all_to_all x1, waiting for transfers between devices, body(): lax.all_to_all(partial_value, ('req', 'exp'), split_axis=0, concat_axis=0...  161 us
    all_to_all x1, waiting for transfers between devices, body(): lax.all_to_all(copies, ('req', 'exp'), split_axis=0, concat_axis=0, tiled...  145 us
    reduce_scatter x1, waiting for transfers between devices, body(): lax.psum_scatter(jnp.dot(attended, out_proj, preferred_element_type=jnp.f...  47.9 us
    all_to_all x1, waiting for transfers between devices, body(): lax.all_to_all(slot_weights, 'req', split_axis=2, concat_axis=0, tiled=True)  37.6 us
    slice x3, local copies, waits for them, and re-layouts, run_slots(): in_rows = grouped[:, slot_num].reshape(sources * capacity, model_width)  28.2 us
    all_to_all x1, starting transfers between devices, body(): lax.all_to_all(copies, ('req', 'exp'), split_axis=0, concat_axis=0, tiled...  20.8 us
    another operation x2, local copies, waits for them, and re-layouts, run_slots(): in_rows = grouped[:, slot_num].reshape(sources * capacity, model_width)  20.1 us
    unnamed x36, local copies, waits for them, and re-layouts  15.9 us
  transfers between devices with their start and end apart: 7, of which 5 were waited for; matrix products, arithmetic and copies ran while one was open for 26% of the time, Pallas kernels for 0%

commit v1 on v0

--- a/solution.py
+++ b/solution.py
@@ -187,7 +187,12 @@
         result_rows.reshape(tok_dev, topk_count, model_width) * gate_values[:, :, None], axis=1
     )
     layer_out = (residual + mixture).astype(jnp.bfloat16)
-    spread_slots = lax.all_to_all(slot_weights, "req", split_axis=2, concat_axis=0, tiled=True)
+    spread_slots = jnp.concatenate(
+        lax.all_to_all(
+            jnp.stack(jnp.split(slot_weights, lax.axis_size("req"), axis=2)), "req", 0, 0
+        ),
+        axis=0,
+    )
     replica_onehot = new_replicas[:, None] == slot_range[None, :]
     source_slot = jnp.sum(jnp.where(replica_onehot, slot_of[None, :], 0), axis=1)
     chosen_pieces = jnp.take(spread_slots, source_slot, axis=0)

time: 704 us -> 682 us (0.969)
  waiting for transfers between devices: 396 us -> 379 us
    all_to_all x1, waiting for transfers between devices: 37.6 us -> 12 us  [body(): lax.all_to_all(jnp.stack(jnp.split(slot_weights, lax.axis_size('req'), ax...]
    unnamed x36 -> x80, local copies, waits for them, and re-layouts: 15.9 us -> 24.2 us
    all_to_all x1, waiting for transfers between devices: 145 us -> 153 us  [body(): lax.all_to_all(copies, ('req', 'exp'), split_axis=0, concat_axis=0, tiled...]
    all_to_all x2 -> x0, local copies, waits for them, and re-layouts: 8.24 us -> none  [body(): lax.all_to_all(slot_weights, 'req', split_axis=2, concat_axis=0, tiled=True)]
where the time goes in v1:
time: 682 us; the launch traced here: 671 us
  waiting for transfers between devices  379 us (56%)
  local copies, waits for them, and re-layouts  146 us (21%)
  starting transfers between devices  57.7 us (8%)
  other arithmetic  41.6 us (6%)
  matrix products  31.6 us (5%)
  between operations  15.4 us (2%)
    all_to_all x1, waiting for transfers between devices, body(): lax.all_to_all(partial_value, ('req', 'exp'), split_axis=0, concat_axis=0...  161 us
    all_to_all x1, waiting for transfers between devices, body(): lax.all_to_all(copies, ('req', 'exp'), split_axis=0, concat_axis=0, tiled...  153 us
    reduce_scatter x1, waiting for transfers between devices, body(): lax.psum_scatter(jnp.dot(attended, out_proj, preferred_element_type=jnp.f...  47.9 us
    slice x3, local copies, waits for them, and re-layouts, run_slots(): in_rows = grouped[:, slot_num].reshape(sources * capacity, model_width)  28.2 us
    unnamed x80, local copies, waits for them, and re-layouts  24.2 us
    another operation x2, local copies, waits for them, and re-layouts, run_slots(): in_rows = grouped[:, slot_num].reshape(sources * capacity, model_width)  20.1 us
    all_to_all x1, starting transfers between devices, body(): lax.all_to_all(copies, ('req', 'exp'), split_axis=0, concat_axis=0, tiled...  14.5 us
    convert_element_type x1, local copies, waits for them, and re-layouts, body(): run_slots(inbox, slot_weights, capacity).astype(jnp.bfloat16)  14 us
  transfers between devices with their start and end apart: 7, of which 5 were waited for; matrix products, arithmetic and copies ran while one was open for 26% of the time, Pallas kernels for 0%

profile of v1, /device:TPU:74, one launch (start us, length us, event | category | flops | bytes accessed | tf_op | source)
XLA Modules:
  0.0 671.4 jit_solution(14654601805482080056)
XLA Ops:
  9.9 8.5 %all-to-all-start = ((bf16[32,2,1,1024]{3,1,2,0:T(2,128)(2,1)}), bf16[32,2,1,1024]{3,1,2,0:T(2,128)(2,1)S(1)}, u32[]{:S(2)}, u32[]{:S(2)}) async-start(bf16[32,2,1,1024]{3,1,2,0:T(2,128)(2,1)} %maximum_bitcast_fusion), calls=%async_computation | async-start | bytes 262144 | tf_op jit(solution)/shard_map/all_to_all | solution.py:110
  51.9 8.3 %all-to-all-start.1 = ((bf16[32,2,1,1024]{3,1,2,0:T(2,128)(2,1)}), bf16[32,2,1,1024]{3,1,2,0:T(2,128)(2,1)S(1)}, u32[]{:S(2)}, u32[]{:S(2)}) async-start(bf16[32,2,1,1024]{3,1,2,0:T(2,128)(2,1)} %broadcast_select_fusion.1), calls=%async_computation.1 | async-start | bytes 262144 | tf_op jit(solution)/shard_map/all_to_all | solution.py:114
  60.4 4.9 all-to-all-done.1
  65.3 8.5 %all-to-all-start.4 = ((bf16[32,2,3,64,256]{4,3,2,1,0:T(8,128)(2,1)}), bf16[32,2,3,64,256]{4,3,2,1,0:T(8,128)(2,1)}, u32[]{:S(2)}, u32[]{:S(2)}) async-start(bf16[32,2,3,64,256]{4,3,2,1,0:T(8,128)(2,1)} %copy-done.3), calls=%async_computation.5 | async-start | bytes 12582912 | tf_op jit(solution)/shard_map/all_to_all | solution.py:191
  82.7 47.9 %reduce-scatter.2.cloned.1.call-done = f32[64,2048]{1,0:T(8,128)} async-done(((f32[256,2048]{1,0:T(8,128)}), f32[64,2048]{1,0:T(8,128)}) %reduce-scatter.2.cloned.1.call-update) | async-done | bytes 524304 | tf_op jit(solution)/shard_map/reduce_scatter | solution.py:141
  133.0 5.6 scatter_custom_fusion
  138.6 5.1 broadcast_in_dim.198
  143.7 12.0 %all-to-all-done.4 = bf16[32,2,3,64,256]{4,3,2,1,0:T(8,128)(2,1)} async-done(((bf16[32,2,3,64,256]{4,3,2,1,0:T(8,128)(2,1)}), bf16[32,2,3,64,256]{4,3,2,1,0:T(8,128)(2,1)}, u32[]{:S(2)}, u32[]{:S(2)}) %all-to-all-start.4) | async-done | bytes 6291488 | tf_op jit(solution)/shard_map/all_to_all | solution.py:191
  155.7 8.1 %broadcast_in_dim.199 = bf16[32,4,20,2048]{3,2,1,0:T(8,128)(2,1)} broadcast(bf16[32,20,2048]{2,1,0:T(8,128)(2,1)} %broadcast_in_dim.198), dimensions={0,2,3} | broadcast | bytes 13107200 | tf_op jit(solution)/shard_map/broadcast_in_dim | solution.py:170
  163.8 14.5 %all-to-all-start.2 = ((bf16[128,20,2048]{2,1,0:T(8,128)(2,1)}), bf16[128,20,2048]{2,1,0:T(8,128)(2,1)}, u32[]{:S(2)}, u32[]{:S(2)}) async-start(bf16[128,20,2048]{2,1,0:T(8,128)(2,1)} %bitcast.182), calls=%async_computation.3 | async-start | bytes 25165824 | tf_op jit(solution)/shard_map/all_to_all | solution.py:174
  178.6 5.2 gather_fusion.2
  187.7 153.2 %all-to-all-done.2 = bf16[128,20,2048]{2,1,0:T(8,128)(2,1)} async-done(((bf16[128,20,2048]{2,1,0:T(8,128)(2,1)}), bf16[128,20,2048]{2,1,0:T(8,128)(2,1)}, u32[]{:S(2)}, u32[]{:S(2)}) %all-to-all-start.2) | async-done | bytes 10485792 | tf_op jit(solution)/shard_map/all_to_all | solution.py:174
  340.9 6.8 %all-to-all-start.5 = ((bf16[32,3,64,256]{3,2,1,0:T(8,128)(2,1)}), bf16[32,3,64,256]{3,2,1,0:T(8,128)(2,1)}, u32[]{:S(2)}, u32[]{:S(2)}) async-start(bf16[32,3,64,256]{3,2,1,0:T(8,128)(2,1)} %broadcast_select_fusion), calls=%async_computation.6 | async-start | bytes 6291456 | tf_op jit(solution)/shard_map/all_to_all | solution.py:199
  347.7 12.7 %copy.112 = bf16[128,20,2048]{2,0,1:T(8,128)(2,1)} copy(bf16[128,20,2048]{2,1,0:T(8,128)(2,1)} %all-to-all-done.2) | data formatting | bytes 20971520 | tf_op jit(solution)/shard_map/all_to_all | solution.py:174
  360.4 10.2 %fusion.65 = (bf16[128,1,10,2048]{3,0,2,1:T(8,128)(2,1)}, bf16[128,1,10,2048]{3,0,2,1:T(8,128)(2,1)}) fusion(bf16[128,2,10,2048]{3,0,2,1:T(8,128)(2,1)} %bitcast.183), kind=kLoop, calls=%fused_computation.166 | loop fusion | bytes 20971520 | tf_op jit(solution)/shard_map/slice | solution.py:48
  370.6 9.0 %copy.113 = bf16[128,1,10,2048]{3,2,0,1:T(8,128)(2,1)} copy(bf16[128,1,10,2048]{3,0,2,1:T(8,128)(2,1)} %get-tuple-element.13) | data formatting | bytes 10485760 | tf_op jit(solution)/shard_map/slice | solution.py:48
  379.6 10.0 %reshape_squeeze.6 = bf16[1280,2048]{1,0:T(8,128)(2,1)} reshape(bf16[128,1,10,2048]{3,2,0,1:T(8,128)(2,1)} %copy.113) | data formatting | bytes 10485760 | tf_op jit(solution)/shard_map/reshape;squeeze | solution.py:48
  389.6 4.5 fusion.17
  397.3 9.0 %copy.115 = bf16[128,1,10,2048]{3,2,0,1:T(8,128)(2,1)} copy(bf16[128,1,10,2048]{3,0,2,1:T(8,128)(2,1)} %get-tuple-element.14) | data formatting | bytes 10485760 | tf_op jit(solution)/shard_map/slice | solution.py:48
  406.3 10.1 %reshape_squeeze.7 = bf16[1280,2048]{1,0:T(8,128)(2,1)} reshape(bf16[128,1,10,2048]{3,2,0,1:T(8,128)(2,1)} %copy.115) | data formatting | bytes 10485760 | tf_op jit(solution)/shard_map/reshape;squeeze | solution.py:48
  416.4 4.5 fusion.14
  424.1 5.0 convert_bitcast_fusion.1
  429.1 5.2 convert_bitcast_fusion
  434.3 9.0 %pad_maximum_fusion = bf16[128,2,10,2048]{3,0,2,1:T(8,128)(2,1)} fusion(bf16[128,1,10,2048]{3,0,2,1:T(8,128)(2,1)} %convert_bitcast_fusion, bf16[128,1,10,2048]{3,0,2,1:T(8,128)(2,1)} %convert_bitcast_fusion.1), kind=kLoop, calls=%fused_computation.6 | loop fusion | flops 5242880 | bytes 20971520 | tf_op jit(solution)/shard_map/stack | solution.py:59
  443.3 14.0 %copy.117 = bf16[128,20,2048]{2,1,0:T(8,128)(2,1)} copy(bf16[128,20,2048]{2,0,1:T(8,128)(2,1)} %bitcast.184) | data formatting | bytes 20971520 | tf_op jit(solution)/shard_map/convert_element_type | solution.py:175
  457.3 11.0 %all-to-all-start.3 = ((bf16[128,20,2048]{2,1,0:T(8,128)(2,1)}), bf16[128,20,2048]{2,1,0:T(8,128)(2,1)}, u32[]{:S(2)}, u32[]{:S(2)}) async-start(bf16[128,20,2048]{2,1,0:T(8,128)(2,1)} %copy.117), calls=%async_computation.4 | async-start | bytes 25165824 | tf_op jit(solution)/shard_map/all_to_all | solution.py:176
  468.5 4.0 copy.121
  472.5 160.7 %all-to-all-done.3 = bf16[128,20,2048]{2,1,0:T(8,128)(2,1)} async-done(((bf16[128,20,2048]{2,1,0:T(8,128)(2,1)}), bf16[128,20,2048]{2,1,0:T(8,128)(2,1)}, u32[]{:S(2)}, u32[]{:S(2)}) %all-to-all-start.3) | async-done | bytes 10485792 | tf_op jit(solution)/shard_map/all_to_all | solution.py:176
  633.3 11.1 %convert_reduce_fusion = f32[32,20,2048]{2,1,0:T(8,128)} fusion(bf16[128,20,2048]{2,1,0:T(8,128)(2,1)} %all-to-all-done.3), kind=kLoop, calls=%fused_computation.5 | loop fusion | flops 9175040 | bytes 15728640 | tf_op jit(solution)/shard_map/reduce_sum | solution.py:179
  644.4 6.8 %reshape.365 = f32[640,2048]{1,0:T(8,128)} reshape(f32[32,20,2048]{2,1,0:T(8,128)} %convert_reduce_fusion) | data formatting | bytes 10485760 | tf_op jit(solution)/shard_map/reshape | solution.py:185
  651.2 8.1 %gather_fusion.1 = f32[512,2048]{1,0:T(8,128)} fusion(f32[640,2048]{1,0:T(8,128)} %reshape.365, s32[1024]{0:T(1024)S(1)} %pad_clamp_fusion.1), kind=kCustom, calls=%fused_computation.1 | custom fusion | bytes 8390656 | tf_op jit(solution)/shard_map/jit(_take)/gather | solution.py:185
  659.3 4.0 fusion.2
  (161 shorter events, 58.4 us)
Async XLA Ops:
  7.2 71.4 %copy-start = (bf16[512,2048]{1,0:T(8,128)(2,1)S(1)}, bf16[512,2048]{1,0:T(8,128)(2,1)}, u32[]{:S(2)}) copy-start(bf16[512,2048]{1,0:T(8,128)(2,1)} %param.27) | copy-start | bytes 6291460
  9.9 40.3 %all-to-all-start = ((bf16[32,2,1,1024]{3,1,2,0:T(2,128)(2,1)}), bf16[32,2,1,1024]{3,1,2,0:T(2,128)(2,1)S(1)}, u32[]{:S(2)}, u32[]{:S(2)}) async-start(bf16[32,2,1,1024]{3,1,2,0:T(2,128)(2,1)} %maximum_bitcast_fusion), calls=%async_computation | async-start | bytes 262144 | tf_op jit(solution)/shard_map/all_to_all | solution.py:110
  20.2 4.2 copy-start.11
  26.9 16.0 %copy-start.2 = (bf16[2,3,2048,256]{3,2,1,0:T(8,128)(2,1)S(1)}, bf16[2,3,2048,256]{3,2,1,0:T(8,128)(2,1)}, u32[]{:S(2)}) copy-start(bf16[2,3,2048,256]{3,2,1,0:T(8,128)(2,1)} %param.33) | copy-start | bytes 18874372
  27.0 19.0 %copy-start.14 = (pred[4]{0:T(512)(128)(4,1)S(1)}, pred[4]{0:T(512)(128)(4,1)}, u32[]{:S(2)}) copy-start(pred[4]{0:T(512)(128)(4,1)} %compare_bitcast_fusion) | copy-start | bytes 16
  27.0 19.0 %copy-start.16 = (s32[4]{0:T(128)S(1)}, s32[4]{0:T(128)}, u32[]{:S(2)}) copy-start(s32[4]{0:T(128)} %fusion.52) | copy-start | bytes 52
  27.0 19.1 %copy-start.15 = (s32[64]{0:T(128)S(1)}, s32[64]{0:T(128)}, u32[]{:S(2)}) copy-start(s32[64]{0:T(128)} %reshape.354) | copy-start | bytes 772
  27.0 19.1 %copy-start.13 = (f32[64]{0:T(128)S(1)}, f32[64]{0:T(128)}, u32[]{:S(2)}) copy-start(f32[64]{0:T(128)} %negate_power_fusion) | copy-start | bytes 772
  28.1 18.6 %copy-start.17 = (f32[128]{0:T(128)S(1)}, f32[128]{0:T(128)}, u32[]{:S(2)}) copy-start(f32[128]{0:T(128)} %param.22) | copy-start | bytes 1540
  28.1 18.6 %copy-start.18 = (f32[128]{0:T(128)S(1)}, f32[128]{0:T(128)}, u32[]{:S(2)}) copy-start(f32[128]{0:T(128)} %param.21) | copy-start | bytes 1540
  42.0 6.2 copy-start.12
  43.4 2.7 copy-start.3
  51.9 13.3 %all-to-all-start.1 = ((bf16[32,2,1,1024]{3,1,2,0:T(2,128)(2,1)}), bf16[32,2,1,1024]{3,1,2,0:T(2,128)(2,1)S(1)}, u32[]{:S(2)}, u32[]{:S(2)}) async-start(bf16[32,2,1,1024]{3,1,2,0:T(2,128)(2,1)} %broadcast_select_fusion.1), calls=%async_computation.1 | async-start | bytes 262144 | tf_op jit(solution)/shard_map/all_to_all | solution.py:114
  65.3 90.4 %all-to-all-start.4 = ((bf16[32,2,3,64,256]{4,3,2,1,0:T(8,128)(2,1)}), bf16[32,2,3,64,256]{4,3,2,1,0:T(8,128)(2,1)}, u32[]{:S(2)}, u32[]{:S(2)}) async-start(bf16[32,2,3,64,256]{4,3,2,1,0:T(8,128)(2,1)} %copy-done.3), calls=%async_computation.5 | async-start | bytes 12582912 | tf_op jit(solution)/shard_map/all_to_all | solution.py:191
  73.8 56.8 %reduce-scatter.2.cloned.1.call-start = ((), (), s32[]{:S(2)}) async-start(), calls=%async_computation.7 | async-start | bytes 2621440 | tf_op jit(solution)/shard_map/reduce_scatter | solution.py:141
  76.8 3.8 copy-start.9
  76.8 5.6 copy-start.19
  76.8 53.8 %copy-start.7 = (bf16[64,2048]{1,0:T(8,128)(2,1)S(1)}, bf16[64,2048]{1,0:T(8,128)(2,1)}, u32[]{:S(2)}) copy-start(bf16[64,2048]{1,0:T(8,128)(2,1)} %param.17) | copy-start | bytes 786436
  76.8 55.0 %copy-start.8 = (f32[2048]{0:T(1024)S(1)}, f32[2048]{0:T(1024)}, u32[]{:S(2)}) copy-start(f32[2048]{0:T(1024)} %param.28) | copy-start | bytes 24580
  163.8 14.5 %copy-start.20 = (s32[32]{0:T(128)S(1)}, s32[32]{0:T(128)}, u32[]{:S(2)}) copy-start(s32[32]{0:T(128)} %param.32) | copy-start | bytes 388
  163.8 177.0 %all-to-all-start.2 = ((bf16[128,20,2048]{2,1,0:T(8,128)(2,1)}), bf16[128,20,2048]{2,1,0:T(8,128)(2,1)}, u32[]{:S(2)}, u32[]{:S(2)}) async-start(bf16[128,20,2048]{2,1,0:T(8,128)(2,1)} %bitcast.182), calls=%async_computation.3 | async-start | bytes 25165824 | tf_op jit(solution)/shard_map/all_to_all | solution.py:174
  340.9 116.4 %all-to-all-start.5 = ((bf16[32,3,64,256]{3,2,1,0:T(8,128)(2,1)}), bf16[32,3,64,256]{3,2,1,0:T(8,128)(2,1)}, u32[]{:S(2)}, u32[]{:S(2)}) async-start(bf16[32,3,64,256]{3,2,1,0:T(8,128)(2,1)} %broadcast_select_fusion), calls=%async_computation.6 | async-start | bytes 6291456 | tf_op jit(solution)/shard_map/all_to_all | solution.py:199
  389.6 4.5 copy-start.4
  416.4 4.5 copy-start.5
  457.3 11.1 %copy-start.10 = (f32[64,8]{0,1:T(8,128)S(1)}, f32[64,8]{0,1:T(8,128)}, u32[]{:S(2)}) copy-start(f32[64,8]{0,1:T(8,128)} %param.30) | copy-start | bytes 6148
  457.3 175.9 %all-to-all-start.3 = ((bf16[128,20,2048]{2,1,0:T(8,128)(2,1)}), bf16[128,20,2048]{2,1,0:T(8,128)(2,1)}, u32[]{:S(2)}, u32[]{:S(2)}) async-start(bf16[128,20,2048]{2,1,0:T(8,128)(2,1)} %copy.117), calls=%async_computation.4 | async-start | bytes 25165824 | tf_op jit(solution)/shard_map/all_to_all | solution.py:176
  651.2 12.2 %copy-start.6 = (f32[64,2048]{1,0:T(8,128)S(1)}, f32[64,2048]{1,0:T(8,128)}, u32[]{:S(2)}) copy-start(f32[64,2048]{1,0:T(8,128)} %reduce-scatter.2.cloned.1.call-done) | copy-start | bytes 1572868
  651.2 12.9 %copy-start.1 = (bf16[512,2048]{1,0:T(8,128)(2,1)S(1)}, bf16[512,2048]{1,0:T(8,128)(2,1)}, u32[]{:S(2)}) copy-start(bf16[512,2048]{1,0:T(8,128)(2,1)} %param.27) | copy-start | bytes 6291460
Sparse Core Ops, SparseCore 0:
  80.7 49.7 reduce-scatter.1
